TPU v7x, 32 devices: a whole 2x2x4 slice. The times are simulated.
32 devices in a mesh: hot: 4 (over y, x), tt: 8 (over z, core).
Axes of the slice: x: 2, y: 2, z: 4, core: 2. Of those that a mesh axis runs over, the one named last changes fastest.
Arguments:
- hot_table: float32 [1024, 256], P('hot'), may hold values from -1.5 to 1.5
- hot_accum: float32 [1024], P('hot'), may hold values from 0.05 to 1
- hot_owner: int32 [8192, 1], P(('hot', 'tt')), may hold values from 0 to 3; in each aligned block of 256 rows (0 to 255, 256 to 511, ...) at most 128 rows name the same one
- hot_row: int32 [32, 256], P(('hot', 'tt')), may hold values from 0 to 255
- hot_bag: int32 [32, 256], P(('hot', 'tt')), may hold values from 0 to 63, never falling along the last dimension, each value on 1 to 12 neighbouring positions
- cold_owner: int32 [16384, 1], P(('hot', 'tt')), may hold values from 0 to 7; in each aligned block of 512 rows (0 to 511, 512 to 1023, ...) at most 128 rows name the same one
- first_index: int32 [32, 512], P(('hot', 'tt')), may hold values from 0 to 127
- mid_index: int32 [32, 512], P(('hot', 'tt')), may hold values from 0 to 63
- last_index: int32 [32, 512], P(('hot', 'tt')), may hold values from 0 to 63
- cold_bag: int32 [32, 512], P(('hot', 'tt')), may hold values from 0 to 63, never falling along the last dimension, each value on 1 to 24 neighbouring positions
- core_first: float32 [1024, 256], P('tt'), may hold values from -1 to 1
- core_mid: bfloat16 [64, 8192], replicated, may hold values from -1 to 1
- core_last: bfloat16 [64, 128], replicated, may hold values from -6 to 6
- bag_grads: bfloat16 [2048, 256], P(('hot', 'tt')), may hold values from -6 to 6
Outputs:
- pooled: float32 [2048, 256], P(('hot', 'tt'))
- new_table: float32 [1024, 256], P('hot')
- new_accum: float32 [1024], P('hot')
- new_first: float32 [1024, 256], P('tt')
Inputs may be any that keep to these rules, and one draw needn't show every extreme that they name: `hot_owner`: among the 256 hot lookups of one device no owner appears more than 128 times; some owner appears exactly that often. `cold_owner`: among the 512 cold lookups of one device no owner appears more than 128 times; some owner appears exactly that often. `hot_bag`: never falling along a device's lookups; every bag of a device has at least one hot lookup. `cold_bag`: never falling along a device's lookups; every bag of a device has at least one cold lookup.
All inputs are finite; a program needn't handle non-finite values.
Results may differ from a plain program's by a relative error of at most 0.005.
Values may be sent and summed in bfloat16 or wider, within the bound.
No kernel may reach another device: no remote copies, remote signals or barrier semaphores. Data moves between devices by JAX's collectives and lax.ppermute only.
A program may use at most 64 MiB of HBM per device.

v0:
```python
import math
import jax
import jax.numpy as jnp
from jax import lax
from jax.sharding import PartitionSpec as P

E1 = 8
E2 = 8
E3 = 4
RANK = 32


def slots_of(owners, peer_count):
    chosen = (owners[:, None] == jnp.arange(peer_count, dtype=jnp.int32)[None, :]).astype(jnp.int32)
    before = jnp.cumsum(chosen, axis=0) - chosen
    return jnp.sum(before * chosen, axis=1)


def slot_source(slot_keys, total_slots):
    lookups = slot_keys.shape[0]
    empty = jnp.full((total_slots,), lookups, jnp.int32)
    return empty.at[slot_keys].set(jnp.arange(lookups, dtype=jnp.int32))


def packed(values, source, fill_value):
    return jnp.take(values, source, axis=0, mode="fill", fill_value=fill_value)


def owner_sum(targets, values, held, precision):
    block_rows = math.gcd(held, 512)
    starts = jnp.arange(held // block_rows, dtype=jnp.int32) * block_rows
    offsets = jnp.arange(block_rows, dtype=jnp.int32)

    def owner_one_block(start):
        picks = ((start + offsets)[:, None] == targets[None, :]).astype(values.dtype)
        return jnp.dot(picks, values, precision=precision, preferred_element_type=jnp.float32)

    return lax.map(owner_one_block, starts).reshape(held, values.shape[1])


def adagrad(table_part, accum_part, grad_part):
    accum_next = accum_part + jnp.mean(grad_part * grad_part, axis=1)
    return (table_part - 0.1 * grad_part / (jnp.sqrt(accum_next)[:, None] + 1e-08), accum_next)


def rank_maps(core_mid, core_last, middle, lasts):
    lookups = middle.shape[0]
    block_rows = math.gcd(lookups, 128)

    def rank_one_block(indices):
        mid_part, last_part = indices
        mid_cores = core_mid[mid_part].reshape(-1, RANK, E2, RANK)
        last_cores = core_last[last_part].reshape(-1, RANK, E3)
        made = jnp.einsum(
            "nawb,nbe->nawe", mid_cores, last_cores, preferred_element_type=jnp.float32
        )
        return made.astype(jnp.bfloat16).reshape(-1, RANK * E2 * E3)

    blocks = lax.map(
        rank_one_block, (middle.reshape(-1, block_rows), lasts.reshape(-1, block_rows))
    )
    return blocks.reshape(lookups, RANK * E2 * E3)


def local(
    hot_table,
    hot_accum,
    hot_owner,
    hot_row,
    hot_bag,
    cold_owner,
    first_index,
    mid_index,
    last_index,
    cold_bag,
    core_first,
    core_mid,
    core_last,
    bag_grads,
):
    rows_held = hot_table.shape[0]
    feature_width = hot_table.shape[1]
    tail_width = feature_width // E1
    bag_count = bag_grads.shape[0]
    bag_range = jnp.arange(bag_count, dtype=jnp.int32)
    hot_peers = lax.axis_size("hot")
    hot_lookups = hot_owner.shape[0]
    hot_cap = 2 * hot_lookups // hot_peers
    row_owner = hot_owner[:, 0]
    row_key = row_owner * hot_cap + slots_of(row_owner, hot_peers)
    row_source = slot_source(row_key, hot_peers * hot_cap)
    request = packed(hot_row[0], row_source, -1).reshape(hot_peers, hot_cap)
    wanted = lax.all_to_all(request, "hot", split_axis=0, concat_axis=0, tiled=True)
    picked = hot_table[jnp.maximum(wanted, 0)].astype(jnp.bfloat16)
    replies = lax.all_to_all(picked, "hot", split_axis=0, concat_axis=0, tiled=True)
    served = wanted
    hot_rows = replies.reshape(-1, feature_width)[row_key]
    hot_pick = (hot_bag[0][:, None] == bag_range[None, :]).astype(jnp.bfloat16)
    hot_cot = jnp.dot(hot_pick, bag_grads, preferred_element_type=jnp.float32).astype(jnp.bfloat16)
    sending = packed(hot_cot, row_source, 0).reshape(hot_peers, hot_cap, feature_width)
    received = lax.all_to_all(sending, "hot", split_axis=0, concat_axis=0, tiled=True)
    row_grad = owner_sum(served.reshape(-1), received.reshape(-1, feature_width), rows_held, None)
    total_grad = lax.psum(row_grad, "tt")
    new_table, new_accum = adagrad(hot_table, hot_accum, total_grad)
    slices_held = core_first.shape[0]
    tt_peers = lax.axis_size("tt")
    cold_lookups = cold_owner.shape[0]
    cold_cap = 2 * cold_lookups // tt_peers
    slice_owner = cold_owner[:, 0]
    slice_key = slice_owner * cold_cap + slots_of(slice_owner, tt_peers)
    slice_source = slot_source(slice_key, tt_peers * cold_cap)
    maps = rank_maps(core_mid, core_last, mid_index[0], last_index[0])
    cold_pick = (cold_bag[0][:, None] == bag_range[None, :]).astype(jnp.bfloat16)
    cold_cot = jnp.dot(cold_pick, bag_grads, preferred_element_type=jnp.float32).astype(
        jnp.bfloat16
    )
    slice_request = packed(first_index[0], slice_source, -1).reshape(tt_peers, cold_cap)
    wanted = lax.all_to_all(slice_request, "tt", split_axis=0, concat_axis=0, tiled=True)
    slices = core_first[jnp.maximum(wanted, 0)].astype(jnp.bfloat16)
    back = lax.all_to_all(slices, "tt", split_axis=0, concat_axis=0, tiled=True)
    slices = back.reshape(-1, E1 * RANK)[slice_key].reshape(cold_lookups, E1, RANK)
    maps_three = maps.reshape(cold_lookups, RANK, tail_width)
    cold_rows = jnp.einsum("kea,kaj->kej", slices, maps_three, preferred_element_type=jnp.float32)
    cold_rows = cold_rows.astype(jnp.bfloat16).reshape(cold_lookups, feature_width)
    local_terms = jnp.einsum(
        "kej,kaj->kea",
        cold_cot.reshape(cold_lookups, E1, tail_width),
        maps_three,
        preferred_element_type=jnp.float32,
    )
    grad_out = packed(local_terms.reshape(cold_lookups, E1 * RANK), slice_source, 0).reshape(
        tt_peers, cold_cap, E1 * RANK
    )
    terms = lax.all_to_all(grad_out, "tt", split_axis=0, concat_axis=0, tiled=True).reshape(
        -1, E1 * RANK
    )
    core_grad = owner_sum(wanted.reshape(-1), terms, slices_held, lax.Precision.HIGHEST)
    core_total = lax.psum(core_grad, "hot")
    new_first = core_first - 0.01 * core_total
    all_rows = jnp.concatenate([hot_rows, cold_rows], axis=0)
    all_picks = jnp.concatenate([hot_pick, cold_pick], axis=0)
    pooled = jnp.einsum("lb,le->be", all_picks, all_rows, preferred_element_type=jnp.float32)
    return (pooled, new_table, new_accum, new_first)


def solution(mesh):
    placed = (
        P("hot", None),
        P("hot"),
        P(("hot", "tt"), None),
        P(("hot", "tt"), None),
        P(("hot", "tt"), None),
        P(("hot", "tt"), None),
        P(("hot", "tt"), None),
        P(("hot", "tt"), None),
        P(("hot", "tt"), None),
        P(("hot", "tt"), None),
        P("tt", None),
        P(),
        P(),
        P(("hot", "tt"), None),
    )
    return jax.shard_map(
        local,
        mesh=mesh,
        in_specs=placed,
        out_specs=(P(("hot", "tt"), None), P("hot", None), P("hot"), P("tt", None)),
        check_vma=False,
    )
```

profile of v0, /device:TPU:0, one launch (start us, length us, event | category | flops | bytes accessed | tf_op | source)
XLA Modules:
  0.0 373.3 jit_solution(5396923980867032876)
XLA Ops:
  17.3 5.2 %all-to-all-start = ((s32[4,1,128]{2,1,0:T(1,128)}), s32[4,1,128]{2,1,0:T(1,128)S(1)}, u32[]{:S(2)}, u32[]{:S(2)}) async-start(s32[4,1,128]{2,1,0:T(1,128)} %bitcast.17), calls=%async_computation | async-start | bytes 4096 | tf_op jit(solution)/shard_map/all_to_all | solution.py:93
  28.7 154.8 %while.2 = (s32[]{:T(128)}, bf16[4,128,1024]{2,1,0:T(8,128)(2,1)S(1)}, s32[4,128]{1,0:T(4,128)}, bf16[64,8192]{1,0:T(8,128)(2,1)}, s32[4,128]{1,0:T(4,128)}, /*index=5*/bf16[64,128]{1,0:T(8,128)(2,1)}, s32[]{:T(128)}) while((s32[]{:T(128)}, bf16[4,128,1024]{2,1,0:T(8,128)(2,1)S(1)}, s32[4,128]{1,0:T(4,128)}, bf16[64,8192]{1,0:T(8,128)(2,1)}, ...), condition=%wide.region_9.10_spmd, body=%wide.region_8.9_spmd.sunk | while | flops 8522498 | bytes 16822392 | solution.py:59
  29.4 6.5 %gather_fusion = bf16[128,8192]{1,0:T(8,128)(2,1)} fusion(bf16[64,8192]{1,0:T(8,128)(2,1)} %get-tuple-element.145, s32[1024]{0:T(1024)S(1)} %pad_clamp_fusion.8), kind=kCustom, calls=%fused_computation.clone.1 | custom fusion | bytes 4194816 | tf_op jit(solution)/shard_map/while/body/eval_jaxpr/gather | solution.py:52
  39.2 11.7 %copy.56 = bf16[128,32,8,32]{3,1,2,0:T(8,128)(2,1)} copy(bf16[128,32,8,32]{0,3,2,1:T(8,128)(2,1)S(1)} %bitcast.108) | data formatting | bytes 4194304 | tf_op jit(solution)/shard_map/while/body/eval_jaxpr/reshape | solution.py:52
  51.9 14.3 %convolution_convert_fusion.5 = bf16[128,32,8,4]{1,3,2,0:T(4,128)(2,1)S(1)} fusion(bf16[128,32,8,32]{3,1,2,0:T(8,128)(2,1)} %copy.56, bf16[128,32,4,1]{1,2,3,0:T(4,128)(2,1)S(1)} %copy.58), kind=kOutput, calls=%fused_computation.12.clone.1 | convolution fusion | flops 8519680 | bytes 2392064 | tf_op jit(solution)/shard_map/while/body/eval_jaxpr/nawb,nbe->nawe/dot_general | solution.py:54
  68.1 6.5 %gather_fusion = bf16[128,8192]{1,0:T(8,128)(2,1)} fusion(bf16[64,8192]{1,0:T(8,128)(2,1)} %get-tuple-element.145, s32[1024]{0:T(1024)S(1)} %pad_clamp_fusion.8), kind=kCustom, calls=%fused_computation.clone.1 | custom fusion | bytes 4194816 | tf_op jit(solution)/shard_map/while/body/eval_jaxpr/gather | solution.py:52
  77.8 11.7 %copy.56 = bf16[128,32,8,32]{3,1,2,0:T(8,128)(2,1)} copy(bf16[128,32,8,32]{0,3,2,1:T(8,128)(2,1)S(1)} %bitcast.108) | data formatting | bytes 4194304 | tf_op jit(solution)/shard_map/while/body/eval_jaxpr/reshape | solution.py:52
  90.6 14.3 %convolution_convert_fusion.5 = bf16[128,32,8,4]{1,3,2,0:T(4,128)(2,1)S(1)} fusion(bf16[128,32,8,32]{3,1,2,0:T(8,128)(2,1)} %copy.56, bf16[128,32,4,1]{1,2,3,0:T(4,128)(2,1)S(1)} %copy.58), kind=kOutput, calls=%fused_computation.12.clone.1 | convolution fusion | flops 8519680 | bytes 2392064 | tf_op jit(solution)/shard_map/while/body/eval_jaxpr/nawb,nbe->nawe/dot_general | solution.py:54
  106.8 6.5 %gather_fusion = bf16[128,8192]{1,0:T(8,128)(2,1)} fusion(bf16[64,8192]{1,0:T(8,128)(2,1)} %get-tuple-element.145, s32[1024]{0:T(1024)S(1)} %pad_clamp_fusion.8), kind=kCustom, calls=%fused_computation.clone.1 | custom fusion | bytes 4194816 | tf_op jit(solution)/shard_map/while/body/eval_jaxpr/gather | solution.py:52
  116.5 11.7 %copy.56 = bf16[128,32,8,32]{3,1,2,0:T(8,128)(2,1)} copy(bf16[128,32,8,32]{0,3,2,1:T(8,128)(2,1)S(1)} %bitcast.108) | data formatting | bytes 4194304 | tf_op jit(solution)/shard_map/while/body/eval_jaxpr/reshape | solution.py:52
  129.3 14.3 %convolution_convert_fusion.5 = bf16[128,32,8,4]{1,3,2,0:T(4,128)(2,1)S(1)} fusion(bf16[128,32,8,32]{3,1,2,0:T(8,128)(2,1)} %copy.56, bf16[128,32,4,1]{1,2,3,0:T(4,128)(2,1)S(1)} %copy.58), kind=kOutput, calls=%fused_computation.12.clone.1 | convolution fusion | flops 8519680 | bytes 2392064 | tf_op jit(solution)/shard_map/while/body/eval_jaxpr/nawb,nbe->nawe/dot_general | solution.py:54
  145.5 6.5 %gather_fusion = bf16[128,8192]{1,0:T(8,128)(2,1)} fusion(bf16[64,8192]{1,0:T(8,128)(2,1)} %get-tuple-element.145, s32[1024]{0:T(1024)S(1)} %pad_clamp_fusion.8), kind=kCustom, calls=%fused_computation.clone.1 | custom fusion | bytes 4194816 | tf_op jit(solution)/shard_map/while/body/eval_jaxpr/gather | solution.py:52
  155.2 11.7 %copy.56 = bf16[128,32,8,32]{3,1,2,0:T(8,128)(2,1)} copy(bf16[128,32,8,32]{0,3,2,1:T(8,128)(2,1)S(1)} %bitcast.108) | data formatting | bytes 4194304 | tf_op jit(solution)/shard_map/while/body/eval_jaxpr/reshape | solution.py:52
  168.0 14.3 %convolution_convert_fusion.5 = bf16[128,32,8,4]{1,3,2,0:T(4,128)(2,1)S(1)} fusion(bf16[128,32,8,32]{3,1,2,0:T(8,128)(2,1)} %copy.56, bf16[128,32,4,1]{1,2,3,0:T(4,128)(2,1)S(1)} %copy.58), kind=kOutput, calls=%fused_computation.12.clone.1 | convolution fusion | flops 8519680 | bytes 2392064 | tf_op jit(solution)/shard_map/while/body/eval_jaxpr/nawb,nbe->nawe/dot_general | solution.py:54
  185.8 6.9 %gather_fusion.5 = s32[1024]{0:T(1024)S(1)} fusion(s32[512]{0:T(512)S(1)} %bitcast.106, s32[1024]{0:T(1024)S(1)} %fusion.18), kind=kCustom, calls=%fused_computation.5 | custom fusion | bytes 12288 | tf_op jit(solution)/shard_map/jit(_take)/gather | solution.py:26
  194.1 4.4 %reshape.359 = bf16[512,32,32]{2,1,0:T(8,128)(2,1)} reshape(bf16[4,128,1024]{2,1,0:T(8,128)(2,1)S(1)} %get-tuple-element.66) | data formatting | bytes 2097152 | tf_op jit(solution)/shard_map/reshape;reshape | solution.py:122
  198.4 4.9 %all-to-all-start.2 = ((s32[8,1,128]{2,1,0:T(1,128)}), s32[8,1,128]{2,1,0:T(1,128)S(1)}, u32[]{:S(2)}, u32[]{:S(2)}) async-start(s32[8,1,128]{2,1,0:T(1,128)} %bitcast.28), calls=%async_computation.2 | async-start | bytes 8192 | tf_op jit(solution)/shard_map/all_to_all | solution.py:118
  208.8 4.2 %all-to-all-start.4 = ((bf16[4,128,256]{2,1,0:T(8,128)(2,1)}), bf16[4,128,256]{2,1,0:T(8,128)(2,1)S(1)}, u32[]{:S(2)}, u32[]{:S(2)}) async-start(bf16[4,128,256]{2,1,0:T(8,128)(2,1)} %broadcast_select_fusion.1), calls=%async_computation.4 | async-start | bytes 524288 | tf_op jit(solution)/shard_map/all_to_all | solution.py:101
  213.0 5.4 %all-to-all-done.4 = bf16[4,128,256]{2,1,0:T(8,128)(2,1)S(1)} async-done(((bf16[4,128,256]{2,1,0:T(8,128)(2,1)}), bf16[4,128,256]{2,1,0:T(8,128)(2,1)S(1)}, u32[]{:S(2)}, u32[]{:S(2)}) %all-to-all-start.4) | async-done | bytes 262176 | tf_op jit(solution)/shard_map/all_to_all | solution.py:101
  221.8 4.6 %gather_fusion.6 = bf16[1024,256]{1,0:T(8,128)(2,1)} fusion(f32[128,256]{1,0:T(8,128)S(1)} %copy-done.2, s32[1024]{0:T(1024)S(1)} %broadcast_clamp_fusion), kind=kCustom, calls=%fused_computation.6 | custom fusion | bytes 1052672 | tf_op jit(solution)/shard_map/gather | solution.py:119
  232.7 4.8 %fusion.25 = f32[512,8,32]{2,1,0:T(8,128)S(1)} fusion(bf16[512,8,32]{2,1,0:T(8,128)(2,1)} %copy.36, bf16[512,32,32]{2,1,0:T(8,128)(2,1)} %reshape.359), kind=kOutput, calls=%fused_computation.83 | convolution fusion | flops 8388608 | bytes 1835008 | tf_op jit(solution)/shard_map/kej,kaj->kea/dot_general | solution.py:125
  245.9 4.0 %all-to-all-start.5 = ((f32[8,128,256]{2,1,0:T(8,128)}), f32[8,128,256]{2,1,0:T(8,128)S(1)}, u32[]{:S(2)}, u32[]{:S(2)}) async-start(f32[8,128,256]{2,1,0:T(8,128)} %broadcast_select_fusion), calls=%async_computation.5 | async-start | bytes 2097152 | tf_op jit(solution)/shard_map/all_to_all | solution.py:134
  252.5 63.3 %all-reduce.3.cloned.1.call-done = f32[256,256]{1,0:T(8,128)} async-done(((f32[256,256]{1,0:T(8,128)}), f32[256,256]{1,0:T(8,128)}) %all-reduce.3.cloned.1.call-update) | async-done | bytes 262160 | tf_op jit(solution)/shard_map/psum | solution.py:103
  328.4 35.9 %all-reduce.5.cloned.1.call-done = f32[128,256]{1,0:T(8,128)} async-done(((f32[128,256]{1,0:T(8,128)}), f32[128,256]{1,0:T(8,128)}) %all-reduce.5.cloned.1.call-update) | async-done | bytes 131088 | tf_op jit(solution)/shard_map/psum | solution.py:138
  (137 shorter events, 84.0 us)
Async XLA Ops:
  8.0 175.5 %copy-start = (bf16[64,256]{1,0:T(8,128)(2,1)S(1)}, bf16[64,256]{1,0:T(8,128)(2,1)}, u32[]{:S(2)}) copy-start(bf16[64,256]{1,0:T(8,128)(2,1)} %param.29) | copy-start | bytes 98308
  17.3 181.1 %all-to-all-start = ((s32[4,1,128]{2,1,0:T(1,128)}), s32[4,1,128]{2,1,0:T(1,128)S(1)}, u32[]{:S(2)}, u32[]{:S(2)}) async-start(s32[4,1,128]{2,1,0:T(1,128)} %bitcast.17), calls=%async_computation | async-start | bytes 4096 | tf_op jit(solution)/shard_map/all_to_all | solution.py:93
  28.7 154.8 %copy-start.8 = (s32[1,256]{1,0:T(1,128)S(1)}, s32[1,256]{1,0:T(1,128)}, u32[]{:S(2)}) copy-start(s32[1,256]{1,0:T(1,128)} %param.20) | copy-start | bytes 3076
  39.1 11.7 %copy-start.3 = (bf16[64,128]{1,0:T(8,128)(2,1)S(1)}, bf16[64,128]{1,0:T(8,128)(2,1)}, u32[]{:S(2)}) copy-start(bf16[64,128]{1,0:T(8,128)(2,1)} %get-tuple-element.147) | copy-start | bytes 49156 | tf_op jit(solution)/shard_map/while
  77.8 11.7 %copy-start.3 = (bf16[64,128]{1,0:T(8,128)(2,1)S(1)}, bf16[64,128]{1,0:T(8,128)(2,1)}, u32[]{:S(2)}) copy-start(bf16[64,128]{1,0:T(8,128)(2,1)} %get-tuple-element.147) | copy-start | bytes 49156 | tf_op jit(solution)/shard_map/while
  116.5 11.7 %copy-start.3 = (bf16[64,128]{1,0:T(8,128)(2,1)S(1)}, bf16[64,128]{1,0:T(8,128)(2,1)}, u32[]{:S(2)}) copy-start(bf16[64,128]{1,0:T(8,128)(2,1)} %get-tuple-element.147) | copy-start | bytes 49156 | tf_op jit(solution)/shard_map/while
  155.2 11.7 %copy-start.3 = (bf16[64,128]{1,0:T(8,128)(2,1)S(1)}, bf16[64,128]{1,0:T(8,128)(2,1)}, u32[]{:S(2)}) copy-start(bf16[64,128]{1,0:T(8,128)(2,1)} %get-tuple-element.147) | copy-start | bytes 49156 | tf_op jit(solution)/shard_map/while
  183.5 2.2 copy-start.1
  185.7 17.6 %copy-start.4 = (f32[256,256]{1,0:T(8,128)S(1)}, f32[256,256]{1,0:T(8,128)}, u32[]{:S(2)}) copy-start(f32[256,256]{1,0:T(8,128)} %param.16) | copy-start | bytes 786436
  194.1 27.7 %copy-start.2 = (f32[128,256]{1,0:T(8,128)S(1)}, f32[128,256]{1,0:T(8,128)}, u32[]{:S(2)}) copy-start(f32[128,256]{1,0:T(8,128)} %param.26) | copy-start | bytes 393220
  198.4 10.4 %all-to-all-start.2 = ((s32[8,1,128]{2,1,0:T(1,128)}), s32[8,1,128]{2,1,0:T(1,128)S(1)}, u32[]{:S(2)}, u32[]{:S(2)}) async-start(s32[8,1,128]{2,1,0:T(1,128)} %bitcast.28), calls=%async_computation.2 | async-start | bytes 8192 | tf_op jit(solution)/shard_map/all_to_all | solution.py:118
  203.3 27.3 %copy-start.7 = (s32[1,512]{1,0:T(1,128)S(1)}, s32[1,512]{1,0:T(1,128)}, u32[]{:S(2)}) copy-start(s32[1,512]{1,0:T(1,128)} %param.25) | copy-start | bytes 6148
  208.8 9.6 %all-to-all-start.4 = ((bf16[4,128,256]{2,1,0:T(8,128)(2,1)}), bf16[4,128,256]{2,1,0:T(8,128)(2,1)S(1)}, u32[]{:S(2)}, u32[]{:S(2)}) async-start(bf16[4,128,256]{2,1,0:T(8,128)(2,1)} %broadcast_select_fusion.1), calls=%async_computation.4 | async-start | bytes 524288 | tf_op jit(solution)/shard_map/all_to_all | solution.py:101
  218.4 8.8 %copy-start.5 = (bf16[4,128,256]{2,1,0:T(8,128)(2,1)}, bf16[4,128,256]{2,1,0:T(8,128)(2,1)S(1)}, u32[]{:S(2)}) copy-start(bf16[4,128,256]{2,1,0:T(8,128)(2,1)S(1)} %all-to-all-done.4) | copy-start | bytes 786436
  218.4 8.8 %all-to-all-start.1 = ((bf16[4,128,256]{2,1,0:T(8,128)(2,1)}), bf16[4,128,256]{2,1,0:T(8,128)(2,1)S(1)}, u32[]{:S(2)}, u32[]{:S(2)}) async-start(bf16[4,128,256]{2,1,0:T(8,128)(2,1)} %bitcast.19), calls=%async_computation.1 | async-start | bytes 524288 | tf_op jit(solution)/shard_map/all_to_all | solution.py:95
  227.1 18.8 %all-to-all-start.3 = ((bf16[8,128,256]{2,1,0:T(8,128)(2,1)}), bf16[8,128,256]{2,1,0:T(8,128)(2,1)S(1)}, u32[]{:S(2)}, u32[]{:S(2)}) async-start(bf16[8,128,256]{2,1,0:T(8,128)(2,1)} %bitcast.30), calls=%async_computation.3 | async-start | bytes 1048576 | tf_op jit(solution)/shard_map/all_to_all | solution.py:120
  243.7 6.5 %copy-start.6 = (bf16[4,128,256]{2,1,0:T(8,128)(2,1)S(1)}, bf16[4,128,256]{2,1,0:T(8,128)(2,1)}, u32[]{:S(2)}) copy-start(bf16[4,128,256]{2,1,0:T(8,128)(2,1)} %copy-done.5) | copy-start | bytes 786436
  243.7 73.2 %copy-start.9 = (f32[256]{0:T(256)S(1)}, f32[256]{0:T(256)}, u32[]{:S(2)}) copy-start(f32[256]{0:T(256)} %param.17) | copy-start | bytes 3076
  245.9 76.2 %all-to-all-start.5 = ((f32[8,128,256]{2,1,0:T(8,128)}), f32[8,128,256]{2,1,0:T(8,128)S(1)}, u32[]{:S(2)}, u32[]{:S(2)}) async-start(f32[8,128,256]{2,1,0:T(8,128)} %broadcast_select_fusion), calls=%async_computation.5 | async-start | bytes 2097152 | tf_op jit(solution)/shard_map/all_to_all | solution.py:134
  249.9 66.0 %all-reduce.3.cloned.1.call-start = ((), (), s32[]{:S(2)}) async-start(), calls=%async_computation.6 | async-start | bytes 524288 | tf_op jit(solution)/shard_map/psum | solution.py:103
  251.2 113.1 %all-reduce.5.cloned.1.call-start = ((), (), s32[]{:S(2)}) async-start(), calls=%async_computation.7 | async-start | bytes 262144 | tf_op jit(solution)/shard_map/psum | solution.py:138
Sparse Core Ops, SparseCore 0:
  253.6 62.2 all-reduce.2
Sparse Core Ops, SparseCore 1:
  323.5 40.7 all-reduce.4
where the time goes:
time: 375 us; the launch traced here: 373 us
  local copies, waits for them, and re-layouts  135 us (36%)
  waiting for transfers between devices  110 us (29%)
  matrix products  68.8 us (18%)
  starting transfers between devices  25.2 us (7%)
  other arithmetic  18 us (5%)
  between operations  15.8 us (4%)
    psum x1, waiting for transfers between devices, local(): total_grad = lax.psum(row_grad, 'tt')  63.3 us
    dot_general x4, matrix products, rank_one_block(): jnp.einsum('nawb,nbe->nawe', mid_cores, last_cores, preferred_element_typ...  57 us
    reshape x4, local copies, waits for them, and re-layouts, rank_one_block(): mid_cores = core_mid[mid_part].reshape(-1, RANK, E2, RANK)  46.9 us
    gather x8, local copies, waits for them, and re-layouts, rank_one_block(): mid_cores = core_mid[mid_part].reshape(-1, RANK, E2, RANK)  38.8 us
    psum x1, waiting for transfers between devices, local(): core_total = lax.psum(core_grad, 'hot')  35.9 us
    gather x4, local copies, waits for them, and re-layouts, packed(): return jnp.take(values, source, axis=0, mode='fill', fill_value=fill_value)  15.9 us
  transfers between devices with their start and end apart: 8, of which 6 were waited for; matrix products, arithmetic and copies ran while one was open for 56% of the time, Pallas kernels for 0%

commit v1 on v0

--- a/solution.py
+++ b/solution.py
@@ -100,7 +100,8 @@
     sending = packed(hot_cot, row_source, 0).reshape(hot_peers, hot_cap, feature_width)
     received = lax.all_to_all(sending, "hot", split_axis=0, concat_axis=0, tiled=True)
     row_grad = owner_sum(served.reshape(-1), received.reshape(-1, feature_width), rows_held, None)
-    total_grad = lax.psum(row_grad, "tt")
+    parts = lax.all_gather(row_grad, "tt")
+    total_grad = jnp.sum(parts, axis=0)
     new_table, new_accum = adagrad(hot_table, hot_accum, total_grad)
     slices_held = core_first.shape[0]
     tt_peers = lax.axis_size("tt")

time: 375 us -> 316 us (0.84)
  waiting for transfers between devices: 110 us -> 53.9 us
    psum x1 -> x0, waiting for transfers between devices: 63.3 us -> none  [local(): total_grad = lax.psum(row_grad, 'tt')]
    psum x1, waiting for transfers between devices: 35.9 us -> 0.01 us  [local(): core_total = lax.psum(core_grad, 'hot')]
    all_to_all x1, waiting for transfers between devices: 0.01 us -> 23.4 us  [local(): lax.all_to_all(grad_out, 'tt', split_axis=0, concat_axis=0, tiled=True)]
    all_to_all x1, waiting for transfers between devices: 1.02 us -> 21.3 us  [local(): back = lax.all_to_all(slices, 'tt', split_axis=0, concat_axis=0, tiled=True)]
  transfers between devices with their start and end apart: 8 -> 8, of which waited for: 6 -> 5; matrix products, arithmetic and copies ran while one was open for 56% -> 66% of each run, Pallas kernels for 0% -> 0%
where the time goes in v1:
time: 316 us; the launch traced here: 314 us
  local copies, waits for them, and re-layouts  133 us (42%)
  matrix products  68.5 us (22%)
  waiting for transfers between devices  53.9 us (17%)
  starting transfers between devices  24.8 us (8%)
  other arithmetic  17.9 us (6%)
  between operations  15.8 us (5%)
    dot_general x4, matrix products, rank_one_block(): jnp.einsum('nawb,nbe->nawe', mid_cores, last_cores, preferred_element_typ...  57 us
    reshape x4, local copies, waits for them, and re-layouts, rank_one_block(): mid_cores = core_mid[mid_part].reshape(-1, RANK, E2, RANK)  46.9 us
    gather x8, local copies, waits for them, and re-layouts, rank_one_block(): mid_cores = core_mid[mid_part].reshape(-1, RANK, E2, RANK)  38.8 us
    all_to_all x1, waiting for transfers between devices, local(): lax.all_to_all(grad_out, 'tt', split_axis=0, concat_axis=0, tiled=True)  23.4 us
    all_to_all x1, waiting for transfers between devices, local(): back = lax.all_to_all(slices, 'tt', split_axis=0, concat_axis=0, tiled=True)  21.3 us
    gather x4, local copies, waits for them, and re-layouts, packed(): return jnp.take(values, source, axis=0, mode='fill', fill_value=fill_value)  16.1 us
  transfers between devices with their start and end apart: 8, of which 5 were waited for; matrix products, arithmetic and copies ran while one was open for 66% of the time, Pallas kernels for 0%

profile of v1, /device:TPU:0, one launch (start us, length us, event | category | flops | bytes accessed | tf_op | source)
XLA Modules:
  0.0 314.1 jit_solution(1622539135402379654)
XLA Ops:
  17.3 5.2 %all-to-all-start = ((s32[4,1,128]{2,1,0:T(1,128)}), s32[4,1,128]{2,1,0:T(1,128)S(1)}, u32[]{:S(2)}, u32[]{:S(2)}) async-start(s32[4,1,128]{2,1,0:T(1,128)} %bitcast.17), calls=%async_computation | async-start | bytes 4096 | tf_op jit(solution)/shard_map/all_to_all | solution.py:93
  28.7 154.8 %while.2 = (s32[]{:T(128)}, bf16[4,128,1024]{2,1,0:T(8,128)(2,1)S(1)}, s32[4,128]{1,0:T(4,128)}, bf16[64,8192]{1,0:T(8,128)(2,1)}, s32[4,128]{1,0:T(4,128)}, /*index=5*/bf16[64,128]{1,0:T(8,128)(2,1)}, s32[]{:T(128)}) while((s32[]{:T(128)}, bf16[4,128,1024]{2,1,0:T(8,128)(2,1)S(1)}, s32[4,128]{1,0:T(4,128)}, bf16[64,8192]{1,0:T(8,128)(2,1)}, ...), condition=%wide.region_9.10_spmd, body=%wide.region_8.9_spmd.sunk | while | flops 8522498 | bytes 16822392 | solution.py:59
  29.4 6.5 %gather_fusion = bf16[128,8192]{1,0:T(8,128)(2,1)} fusion(bf16[64,8192]{1,0:T(8,128)(2,1)} %get-tuple-element.145, s32[1024]{0:T(1024)S(1)} %pad_clamp_fusion.8), kind=kCustom, calls=%fused_computation.clone.1 | custom fusion | bytes 4194816 | tf_op jit(solution)/shard_map/while/body/eval_jaxpr/gather | solution.py:52
  39.1 11.7 %copy.56 = bf16[128,32,8,32]{3,1,2,0:T(8,128)(2,1)} copy(bf16[128,32,8,32]{0,3,2,1:T(8,128)(2,1)S(1)} %bitcast.109) | data formatting | bytes 4194304 | tf_op jit(solution)/shard_map/while/body/eval_jaxpr/reshape | solution.py:52
  51.9 14.3 %convolution_convert_fusion.5 = bf16[128,32,8,4]{1,3,2,0:T(4,128)(2,1)S(1)} fusion(bf16[128,32,8,32]{3,1,2,0:T(8,128)(2,1)} %copy.56, bf16[128,32,4,1]{1,2,3,0:T(4,128)(2,1)S(1)} %copy.58), kind=kOutput, calls=%fused_computation.12.clone.1 | convolution fusion | flops 8519680 | bytes 2392064 | tf_op jit(solution)/shard_map/while/body/eval_jaxpr/nawb,nbe->nawe/dot_general | solution.py:54
  68.1 6.5 %gather_fusion = bf16[128,8192]{1,0:T(8,128)(2,1)} fusion(bf16[64,8192]{1,0:T(8,128)(2,1)} %get-tuple-element.145, s32[1024]{0:T(1024)S(1)} %pad_clamp_fusion.8), kind=kCustom, calls=%fused_computation.clone.1 | custom fusion | bytes 4194816 | tf_op jit(solution)/shard_map/while/body/eval_jaxpr/gather | solution.py:52
  77.8 11.7 %copy.56 = bf16[128,32,8,32]{3,1,2,0:T(8,128)(2,1)} copy(bf16[128,32,8,32]{0,3,2,1:T(8,128)(2,1)S(1)} %bitcast.109) | data formatting | bytes 4194304 | tf_op jit(solution)/shard_map/while/body/eval_jaxpr/reshape | solution.py:52
  90.6 14.3 %convolution_convert_fusion.5 = bf16[128,32,8,4]{1,3,2,0:T(4,128)(2,1)S(1)} fusion(bf16[128,32,8,32]{3,1,2,0:T(8,128)(2,1)} %copy.56, bf16[128,32,4,1]{1,2,3,0:T(4,128)(2,1)S(1)} %copy.58), kind=kOutput, calls=%fused_computation.12.clone.1 | convolution fusion | flops 8519680 | bytes 2392064 | tf_op jit(solution)/shard_map/while/body/eval_jaxpr/nawb,nbe->nawe/dot_general | solution.py:54
  106.8 6.5 %gather_fusion = bf16[128,8192]{1,0:T(8,128)(2,1)} fusion(bf16[64,8192]{1,0:T(8,128)(2,1)} %get-tuple-element.145, s32[1024]{0:T(1024)S(1)} %pad_clamp_fusion.8), kind=kCustom, calls=%fused_computation.clone.1 | custom fusion | bytes 4194816 | tf_op jit(solution)/shard_map/while/body/eval_jaxpr/gather | solution.py:52
  116.5 11.7 %copy.56 = bf16[128,32,8,32]{3,1,2,0:T(8,128)(2,1)} copy(bf16[128,32,8,32]{0,3,2,1:T(8,128)(2,1)S(1)} %bitcast.109) | data formatting | bytes 4194304 | tf_op jit(solution)/shard_map/while/body/eval_jaxpr/reshape | solution.py:52
  129.3 14.3 %convolution_convert_fusion.5 = bf16[128,32,8,4]{1,3,2,0:T(4,128)(2,1)S(1)} fusion(bf16[128,32,8,32]{3,1,2,0:T(8,128)(2,1)} %copy.56, bf16[128,32,4,1]{1,2,3,0:T(4,128)(2,1)S(1)} %copy.58), kind=kOutput, calls=%fused_computation.12.clone.1 | convolution fusion | flops 8519680 | bytes 2392064 | tf_op jit(solution)/shard_map/while/body/eval_jaxpr/nawb,nbe->nawe/dot_general | solution.py:54
  145.5 6.5 %gather_fusion = bf16[128,8192]{1,0:T(8,128)(2,1)} fusion(bf16[64,8192]{1,0:T(8,128)(2,1)} %get-tuple-element.145, s32[1024]{0:T(1024)S(1)} %pad_clamp_fusion.8), kind=kCustom, calls=%fused_computation.clone.1 | custom fusion | bytes 4194816 | tf_op jit(solution)/shard_map/while/body/eval_jaxpr/gather | solution.py:52
  155.2 11.7 %copy.56 = bf16[128,32,8,32]{3,1,2,0:T(8,128)(2,1)} copy(bf16[128,32,8,32]{0,3,2,1:T(8,128)(2,1)S(1)} %bitcast.109) | data formatting | bytes 4194304 | tf_op jit(solution)/shard_map/while/body/eval_jaxpr/reshape | solution.py:52
  168.0 14.3 %convolution_convert_fusion.5 = bf16[128,32,8,4]{1,3,2,0:T(4,128)(2,1)S(1)} fusion(bf16[128,32,8,32]{3,1,2,0:T(8,128)(2,1)} %copy.56, bf16[128,32,4,1]{1,2,3,0:T(4,128)(2,1)S(1)} %copy.58), kind=kOutput, calls=%fused_computation.12.clone.1 | convolution fusion | flops 8519680 | bytes 2392064 | tf_op jit(solution)/shard_map/while/body/eval_jaxpr/nawb,nbe->nawe/dot_general | solution.py:54
  183.5 4.4 %reshape.358 = bf16[512,32,32]{2,1,0:T(8,128)(2,1)} reshape(bf16[4,128,1024]{2,1,0:T(8,128)(2,1)S(1)} %get-tuple-element.66) | data formatting | bytes 2097152 | tf_op jit(solution)/shard_map/reshape;reshape | solution.py:123
  189.0 7.1 %gather_fusion.5 = s32[1024]{0:T(1024)S(1)} fusion(s32[512]{0:T(512)S(1)} %bitcast.107, s32[1024]{0:T(1024)S(1)} %fusion.18), kind=kCustom, calls=%fused_computation.5 | custom fusion | bytes 12288 | tf_op jit(solution)/shard_map/jit(_take)/gather | solution.py:26
  196.1 4.4 %fusion.25 = f32[512,8,32]{2,1,0:T(8,128)S(1)} fusion(bf16[512,8,32]{2,1,0:T(8,128)(2,1)S(1)} %copy.36, bf16[512,32,32]{2,1,0:T(8,128)(2,1)} %reshape.358), kind=kOutput, calls=%fused_computation.83 | convolution fusion | flops 8388608 | bytes 1835008 | tf_op jit(solution)/shard_map/kej,kaj->kea/dot_general | solution.py:126
  205.6 4.9 %all-to-all-start.2 = ((s32[8,1,128]{2,1,0:T(1,128)}), s32[8,1,128]{2,1,0:T(1,128)S(1)}, u32[]{:S(2)}, u32[]{:S(2)}) async-start(s32[8,1,128]{2,1,0:T(1,128)} %bitcast.28), calls=%async_computation.2 | async-start | bytes 8192 | tf_op jit(solution)/shard_map/all_to_all | solution.py:119
  211.6 4.3 %all-to-all-done.2 = s32[8,1,128]{2,1,0:T(1,128)S(1)} async-done(((s32[8,1,128]{2,1,0:T(1,128)}), s32[8,1,128]{2,1,0:T(1,128)S(1)}, u32[]{:S(2)}, u32[]{:S(2)}) %all-to-all-start.2) | async-done | bytes 4128 | tf_op jit(solution)/shard_map/all_to_all | solution.py:119
  222.6 23.4 %all-to-all-done.5 = f32[8,128,256]{2,1,0:T(8,128)S(1)} async-done(((f32[8,128,256]{2,1,0:T(8,128)}), f32[8,128,256]{2,1,0:T(8,128)S(1)}, u32[]{:S(2)}, u32[]{:S(2)}) %all-to-all-start.5) | async-done | bytes 1048608 | tf_op jit(solution)/shard_map/all_to_all | solution.py:135
  246.0 4.2 %all-to-all-start.4 = ((bf16[4,128,256]{2,1,0:T(8,128)(2,1)}), bf16[4,128,256]{2,1,0:T(8,128)(2,1)S(1)}, u32[]{:S(2)}, u32[]{:S(2)}) async-start(bf16[4,128,256]{2,1,0:T(8,128)(2,1)} %broadcast_select_fusion.1), calls=%async_computation.4 | async-start | bytes 524288 | tf_op jit(solution)/shard_map/all_to_all | solution.py:101
  251.5 4.1 %all-to-all-done.4 = bf16[4,128,256]{2,1,0:T(8,128)(2,1)S(1)} async-done(((bf16[4,128,256]{2,1,0:T(8,128)(2,1)}), bf16[4,128,256]{2,1,0:T(8,128)(2,1)S(1)}, u32[]{:S(2)}, u32[]{:S(2)}) %all-to-all-start.4) | async-done | bytes 262176 | tf_op jit(solution)/shard_map/all_to_all | solution.py:101
  262.3 4.6 %gather_fusion.6 = bf16[1024,256]{1,0:T(8,128)(2,1)} fusion(f32[128,256]{1,0:T(8,128)S(1)} %copy-done.2, s32[1024]{0:T(1024)S(1)} %broadcast_clamp_fusion), kind=kCustom, calls=%fused_computation.6 | custom fusion | bytes 1052672 | tf_op jit(solution)/shard_map/gather | solution.py:120
  272.6 21.3 %all-to-all-done.3 = bf16[8,128,256]{2,1,0:T(8,128)(2,1)S(1)} async-done(((bf16[8,128,256]{2,1,0:T(8,128)(2,1)}), bf16[8,128,256]{2,1,0:T(8,128)(2,1)S(1)}, u32[]{:S(2)}, u32[]{:S(2)}) %all-to-all-start.3) | async-done | bytes 524320 | tf_op jit(solution)/shard_map/all_to_all | solution.py:121
  (134 shorter events, 80.3 us)
Async XLA Ops:
  8.0 179.9 %copy-start = (bf16[64,256]{1,0:T(8,128)(2,1)S(1)}, bf16[64,256]{1,0:T(8,128)(2,1)}, u32[]{:S(2)}) copy-start(bf16[64,256]{1,0:T(8,128)(2,1)} %param.29) | copy-start | bytes 98308
  17.3 188.2 %all-to-all-start = ((s32[4,1,128]{2,1,0:T(1,128)}), s32[4,1,128]{2,1,0:T(1,128)S(1)}, u32[]{:S(2)}, u32[]{:S(2)}) async-start(s32[4,1,128]{2,1,0:T(1,128)} %bitcast.17), calls=%async_computation | async-start | bytes 4096 | tf_op jit(solution)/shard_map/all_to_all | solution.py:93
  39.1 11.7 %copy-start.3 = (bf16[64,128]{1,0:T(8,128)(2,1)S(1)}, bf16[64,128]{1,0:T(8,128)(2,1)}, u32[]{:S(2)}) copy-start(bf16[64,128]{1,0:T(8,128)(2,1)} %get-tuple-element.147) | copy-start | bytes 49156 | tf_op jit(solution)/shard_map/while
  77.8 11.7 %copy-start.3 = (bf16[64,128]{1,0:T(8,128)(2,1)S(1)}, bf16[64,128]{1,0:T(8,128)(2,1)}, u32[]{:S(2)}) copy-start(bf16[64,128]{1,0:T(8,128)(2,1)} %get-tuple-element.147) | copy-start | bytes 49156 | tf_op jit(solution)/shard_map/while
  116.5 11.7 %copy-start.3 = (bf16[64,128]{1,0:T(8,128)(2,1)S(1)}, bf16[64,128]{1,0:T(8,128)(2,1)}, u32[]{:S(2)}) copy-start(bf16[64,128]{1,0:T(8,128)(2,1)} %get-tuple-element.147) | copy-start | bytes 49156 | tf_op jit(solution)/shard_map/while
  155.2 11.7 %copy-start.3 = (bf16[64,128]{1,0:T(8,128)(2,1)S(1)}, bf16[64,128]{1,0:T(8,128)(2,1)}, u32[]{:S(2)}) copy-start(bf16[64,128]{1,0:T(8,128)(2,1)} %get-tuple-element.147) | copy-start | bytes 49156 | tf_op jit(solution)/shard_map/while
  183.5 4.4 %copy-start.5 = (s32[1,512]{1,0:T(1,128)S(1)}, s32[1,512]{1,0:T(1,128)}, u32[]{:S(2)}) copy-start(s32[1,512]{1,0:T(1,128)} %param.25) | copy-start | bytes 6148
  183.5 5.5 %copy-start.1 = (s32[1,512]{1,0:T(1,128)S(1)}, s32[1,512]{1,0:T(1,128)}, u32[]{:S(2)}) copy-start(s32[1,512]{1,0:T(1,128)} %param.22) | copy-start | bytes 6148
  205.6 14.0 %copy-start.6 = (s32[1,256]{1,0:T(1,128)S(1)}, s32[1,256]{1,0:T(1,128)}, u32[]{:S(2)}) copy-start(s32[1,256]{1,0:T(1,128)} %param.20) | copy-start | bytes 3076
  205.6 10.4 %all-to-all-start.2 = ((s32[8,1,128]{2,1,0:T(1,128)}), s32[8,1,128]{2,1,0:T(1,128)S(1)}, u32[]{:S(2)}, u32[]{:S(2)}) async-start(s32[8,1,128]{2,1,0:T(1,128)} %bitcast.28), calls=%async_computation.2 | async-start | bytes 8192 | tf_op jit(solution)/shard_map/all_to_all | solution.py:119
  211.6 45.0 %copy-start.4 = (f32[256,256]{1,0:T(8,128)S(1)}, f32[256,256]{1,0:T(8,128)}, u32[]{:S(2)}) copy-start(f32[256,256]{1,0:T(8,128)} %param.16) | copy-start | bytes 786436
  216.0 30.1 %all-to-all-start.5 = ((f32[8,128,256]{2,1,0:T(8,128)}), f32[8,128,256]{2,1,0:T(8,128)S(1)}, u32[]{:S(2)}, u32[]{:S(2)}) async-start(f32[8,128,256]{2,1,0:T(8,128)} %broadcast_select_fusion), calls=%async_computation.5 | async-start | bytes 2097152 | tf_op jit(solution)/shard_map/all_to_all | solution.py:135
  219.8 42.5 %copy-start.2 = (f32[128,256]{1,0:T(8,128)S(1)}, f32[128,256]{1,0:T(8,128)}, u32[]{:S(2)}) copy-start(f32[128,256]{1,0:T(8,128)} %param.26) | copy-start | bytes 393220
  246.0 9.6 %all-to-all-start.4 = ((bf16[4,128,256]{2,1,0:T(8,128)(2,1)}), bf16[4,128,256]{2,1,0:T(8,128)(2,1)S(1)}, u32[]{:S(2)}, u32[]{:S(2)}) async-start(bf16[4,128,256]{2,1,0:T(8,128)(2,1)} %broadcast_select_fusion.1), calls=%async_computation.4 | async-start | bytes 524288 | tf_op jit(solution)/shard_map/all_to_all | solution.py:101
  250.2 51.5 %all-reduce.2.cloned.1.call-start = ((), (), s32[]{:S(2)}) async-start(), calls=%async_computation.6 | async-start | bytes 262144 | tf_op jit(solution)/shard_map/psum | solution.py:139
  251.5 51.9 %all-gather.3.cloned.1.call-start = ((), (), s32[]{:S(2)}) async-start(), calls=%async_computation.7 | async-start | bytes 2359296 | tf_op jit(solution)/shard_map/all_gather | solution.py:103
  258.8 8.8 %all-to-all-start.1 = ((bf16[4,128,256]{2,1,0:T(8,128)(2,1)}), bf16[4,128,256]{2,1,0:T(8,128)(2,1)S(1)}, u32[]{:S(2)}, u32[]{:S(2)}) async-start(bf16[4,128,256]{2,1,0:T(8,128)(2,1)} %bitcast.19), calls=%async_computation.1 | async-start | bytes 524288 | tf_op jit(solution)/shard_map/all_to_all | solution.py:95
  267.6 26.3 %all-to-all-start.3 = ((bf16[8,128,256]{2,1,0:T(8,128)(2,1)}), bf16[8,128,256]{2,1,0:T(8,128)(2,1)S(1)}, u32[]{:S(2)}, u32[]{:S(2)}) async-start(bf16[8,128,256]{2,1,0:T(8,128)(2,1)} %bitcast.30), calls=%async_computation.3 | async-start | bytes 1048576 | tf_op jit(solution)/shard_map/all_to_all | solution.py:121
  300.1 5.1 %copy-start.7 = (f32[256]{0:T(256)S(1)}, f32[256]{0:T(256)}, u32[]{:S(2)}) copy-start(f32[256]{0:T(256)} %param.17) | copy-start | bytes 3076
Sparse Core Ops, SparseCore 0:
  254.5 41.5 all-reduce.1
Sparse Core Ops, SparseCore 1:
  256.7 36.8 all-gather.2
